TPU v7x, 512 devices: a whole 4x4x16 slice. The times are simulated.
512 devices in a mesh: sub: 16 (over z), row: 4 (over y), col: 8 (over x, core).
Axes of the slice: x: 4, y: 4, z: 16, core: 2. Of those that a mesh axis runs over, the one named last changes fastest.
Arguments:
- child_factor: float32 [16, 256, 2048], P('sub', None, 'row'), may hold values from -6 to 6
- child_map: int32 [16, 2048], P('sub'), may hold values from 0 to 8191, as said below
- child_len: int32 [16], P('sub'), may hold values from 1 to 2048, 16384 in all
- class_ids: int32 [8192], replicated, may hold values from 0 to 7
- class_kappa: float32 [8], replicated, may hold values from 0.25 to 16
- landmarks: int32 [256], replicated, may hold values from 0 to 1023
- diag_inverse: float32 [2, 512, 512], replicated, as said below
Outputs:
- panel_factor: float32 [2, 512, 16, 512], P(None, 'col', 'sub', 'row')
- landmark_solution: float32 [256, 16, 512], P('col', 'sub', 'row')
Inputs may be any that keep to these rules, and one draw needn't show every extreme that they name: `child_map`: node i of a child maps to parent row 512 a + 128 (i // 512) + u for some block a and some u below 128; the nodes of one child map to distinct rows. `diag_inverse`: each 512 x 512 block is lower triangular with a positive diagonal.
All inputs are finite; a program needn't handle non-finite values. No bound on the sum of `child_len` on one device may be relied on, other than what follows from the above.
Results may differ from a plain program's by a relative error of at most 0.0003.
Values sent between devices are 32-bit elements; how exact they have to be, the bound alone decides.
A program may use at most 64 MiB of HBM per device.

v0:
```python
import jax
import jax.numpy as jnp
from jax import lax
from jax.sharding import PartitionSpec as P

PRECISE = lax.Precision.HIGHEST


def from_root(value, axis, root):
    mine = lax.axis_index(axis) == root
    return lax.psum(jnp.where(mine, value, jnp.zeros_like(value)), axis)


def contract(left_part, right_part, left_dim, right_dim):
    return lax.dot_general(
        left_part,
        right_part,
        (((left_dim,), (right_dim,)), ((), ())),
        precision=PRECISE,
        preferred_element_type=jnp.float32,
    )


def on_device(child_factor, child_map, child_len, class_ids, class_kappa, landmarks, diag_inverse):
    sub_index = lax.axis_index("sub")
    row_index = lax.axis_index("row")
    col_index = lax.axis_index("col")
    sub_count = lax.axis_size("sub")
    row_count = lax.axis_size("row")
    col_count = lax.axis_size("col")
    panels = diag_inverse.shape[0]
    width_panel = diag_inverse.shape[1]
    total_nodes = class_ids.shape[0]
    col_width = width_panel // col_count
    quarter = width_panel // row_count
    quarter_rows = total_nodes // row_count
    local_rows = quarter_rows // sub_count
    blocks_local = local_rows // quarter
    node_quarter = child_factor.shape[2]
    own_cols = (
        jnp.arange(panels, dtype=jnp.int32)[:, None] * width_panel
        + col_index * col_width
        + jnp.arange(col_width, dtype=jnp.int32)[None, :]
    ).reshape(-1)
    node_map = child_map[0]
    node_index = row_index * node_quarter + jnp.arange(node_quarter, dtype=jnp.int32)
    live_factor = jnp.where((node_index < child_len[0])[None, :], child_factor[0], jnp.float32(0.0))
    select = (node_map[:, None] == own_cols[None, :]).astype(jnp.float32)
    reduced = jnp.dot(
        lax.all_gather(live_factor, "row", axis=1, tiled=True), select, precision=PRECISE
    )
    partial_cols = jnp.zeros((node_quarter, own_cols.shape[0]), jnp.float32) - contract(
        live_factor, reduced, 0, 0
    )
    parent = lax.dynamic_slice_in_dim(node_map, row_index * node_quarter, node_quarter)
    target = parent // width_panel * quarter + parent % width_panel - row_index * quarter
    place_rows = (target[:, None] == jnp.arange(quarter_rows, dtype=jnp.int32)[None, :]).astype(
        jnp.float32
    )
    contribution = contract(partial_cols, place_rows, 0, 0)
    front_cols = lax.psum_scatter(contribution, "sub", scatter_dimension=1, tiled=True)
    class_table = (
        class_ids[:, None] == jnp.arange(class_kappa.shape[0], dtype=jnp.int32)[None, :]
    ).astype(jnp.float32)
    coefficient = jnp.sum(class_table * class_kappa[None, :], axis=1) + jnp.float32(4.0)
    local_index = jnp.arange(local_rows, dtype=jnp.int32)
    global_rows = (
        (sub_index * blocks_local + local_index // quarter) * width_panel
        + row_index * quarter
        + local_index % quarter
    )
    coeff_row = jnp.take(coefficient, global_rows)[None, :]
    coeff_col = jnp.take(coefficient, own_cols)[:, None]
    offset_band = global_rows[None, :] - own_cols[:, None]
    end_count = jnp.where(
        (global_rows == 0) | (global_rows == total_nodes - 1), jnp.float32(1.0), jnp.float32(2.0)
    )[None, :]
    band_part = jnp.where(
        offset_band == 0,
        coeff_row * coeff_row + end_count,
        jnp.where(
            jnp.abs(offset_band) == 1,
            -(coeff_row + coeff_col),
            jnp.where(jnp.abs(offset_band) == 2, jnp.float32(1.0), jnp.float32(0.0)),
        ),
    )
    front_cols = front_cols + band_part
    land_count = landmarks.shape[0] // col_count
    chooser = (landmarks[:, None] == own_cols[None, :]).astype(jnp.float32)
    right_side = lax.psum_scatter(
        jnp.dot(chooser, front_cols, precision=PRECISE), "col", scatter_dimension=0, tiled=True
    )
    column_slabs = [slab for slab in front_cols.reshape(panels, col_width, local_rows)]
    inner_index = jnp.arange(width_panel, dtype=jnp.int32)
    block_of_row = global_rows // width_panel
    pieces = []
    for panel_index in range(panels):
        inverse = diag_inverse[panel_index]
        panel_now = contract(
            lax.all_gather(column_slabs[panel_index], "col", axis=0, tiled=True), inverse, 0, 1
        )
        keep_mask = global_rows[:, None] - panel_index * width_panel >= inner_index[None, :]
        panel_now = jnp.where(keep_mask, panel_now, jnp.float32(0.0))
        pieces.append(lax.dynamic_slice_in_dim(panel_now, col_index * col_width, col_width, 1).T)
        for later_panel in range(panel_index + 1, panels):
            owner_sub = later_panel // blocks_local
            whole_block = from_root(
                lax.all_gather(panel_now, "row", axis=0, tiled=True), "sub", owner_sub
            )
            my_slice = lax.dynamic_slice_in_dim(whole_block, col_index * col_width, col_width, 0)
            column_slabs[later_panel] = column_slabs[later_panel] - contract(
                my_slice, panel_now, 1, 1
            )
        owner_sub = panel_index // blocks_local
        gathered = lax.all_gather(right_side, "row", axis=1, tiled=True)
        values = from_root(contract(gathered, inverse, 1, 1), "sub", owner_sub)
        below_update = contract(values, panel_now, 1, 1)
        settled = jnp.tile(
            lax.dynamic_slice_in_dim(values, row_index * quarter, quarter, 1), (1, blocks_local)
        )
        right_side = jnp.where(
            (block_of_row > panel_index)[None, :],
            right_side - below_update,
            jnp.where((block_of_row == panel_index)[None, :], settled, right_side),
        )
    panel_factor = jnp.stack(pieces).reshape(panels, col_width, blocks_local, quarter)
    landmark_solution = right_side.reshape(land_count, blocks_local, quarter)
    return (panel_factor, landmark_solution)


def solution(mesh):
    return jax.shard_map(
        on_device,
        mesh=mesh,
        in_specs=(P("sub", None, "row"), P("sub", None), P("sub"), P(), P(), P(), P()),
        out_specs=(P(None, "col", "sub", "row"), P("col", "sub", "row")),
        check_vma=False,
    )
```

profile of v0, /device:TPU:1, one launch (start us, length us, event | category | flops | bytes accessed | tf_op | source)
XLA Modules:
  0.0 513.7 jit_solution(16760685932046861145)
XLA Ops:
  7.9 1.9 bitcast_select_fusion
  10.7 43.3 %all-gather.3.cloned.1.call-done = f32[256,2048]{1,0:T(8,128)} async-done(((f32[256,512]{1,0:T(8,128)}), f32[256,2048]{1,0:T(8,128)}) %all-gather.3.cloned.1.call-update) | async-done | bytes 2097168 | tf_op jit(solution)/shard_map/all_gather | solution.py:50
  54.0 2.8 fusion.8
  56.8 1.0 convolution_subtract_fusion
  57.9 2.7 fusion
  60.8 1.1 gather_fusion
  62.0 1.1 gather_fusion.1
  63.2 58.0 %reduce-scatter.3.cloned.1.call-done = f32[128,128]{1,0:T(8,128)} async-done(((f32[128,2048]{1,0:T(8,128)}), f32[128,128]{1,0:T(8,128)}) %reduce-scatter.3.cloned.1.call-update) | async-done | bytes 65552 | tf_op jit(solution)/shard_map/reduce_scatter | solution.py:61
  123.2 23.6 %all_gather.19 = f32[512,128]{1,0:T(8,128)S(1)} all-gather(f32[64,128]{1,0:T(8,128)S(1)} %unstack.10), channel_id=1, replica_groups=mesh['sub'=16,'row'=4,'col'=8] {'col'}, dimensions={0}, use_global_device_ids=true | all-gather | bytes 294912 | tf_op jit(solution)/shard_map/all_gather | solution.py:100
  146.8 21.6 %reduce-scatter.5.cloned.1.call-done = f32[32,128]{1,0:T(8,128)} async-done(((f32[256,128]{1,0:T(8,128)}), f32[32,128]{1,0:T(8,128)}) %reduce-scatter.5.cloned.1.call-update) | async-done | bytes 16400 | tf_op jit(solution)/shard_map/reduce_scatter | solution.py:90
  168.4 9.3 %all_gather.22 = f32[32,512]{1,0:T(8,128)S(1)} all-gather(f32[32,128]{1,0:T(8,128)} %reduce-scatter.5.cloned.1.call-done), channel_id=1, replica_groups=mesh['sub'=16,'row'=4,'col'=8] {'row'}, dimensions={1}, use_global_device_ids=true | all-gather | bytes 81920 | tf_op jit(solution)/shard_map/all_gather | solution.py:115
  177.7 1.7 convolution_select_fusion.3
  179.4 2.0 convolution_select_fusion.1
  181.5 123.4 %all-reduce.4.cloned.1.call-done = f32[32,512]{1,0:T(8,128)} async-done(((f32[32,512]{1,0:T(8,128)}), f32[32,512]{1,0:T(8,128)}) %all-reduce.4.cloned.1.call-update) | async-done | bytes 65552 | tf_op jit(solution)/shard_map/psum | solution.py:11
  304.9 1.3 fusion.3
  306.2 9.7 %all_gather.23 = f32[32,512]{1,0:T(8,128)S(1)} all-gather(f32[32,128]{1,0:T(8,128)S(1)} %fusion.3), channel_id=1, replica_groups=mesh['sub'=16,'row'=4,'col'=8] {'row'}, dimensions={1}, use_global_device_ids=true | all-gather | bytes 81920 | tf_op jit(solution)/shard_map/all_gather | solution.py:115
  316.0 1.7 convolution_select_fusion.2
  317.7 27.0 %all-gather.5.cloned.1.call-done = f32[512,512]{1,0:T(8,128)} async-done(((f32[128,512]{1,0:T(8,128)}), f32[512,512]{1,0:T(8,128)}) %all-gather.5.cloned.1.call-update) | async-done | bytes 1048592 | tf_op jit(solution)/shard_map/all_gather | solution.py:108
  344.7 1.1 broadcast_select_fusion
  345.9 133.4 %all-reduce.6.cloned.1.call-done = (f32[512,512]{1,0:T(8,128)}, f32[32,512]{1,0:T(8,128)}) async-done(((f32[512,512]{1,0:T(8,128)}, f32[32,512]{1,0:T(8,128)}), (f32[512,512]{1,0:T(8,128)}, f32[32,512]{1,0:T(8,128)})) %all-reduce.6.cloned.1.call-update) | async-done | bytes 1114128 | tf_op jit(solution)/shard_map/psum | solution.py:11
  479.3 1.3 convolution_subtract_fusion.1
  480.6 23.2 %all_gather.21 = f32[512,128]{1,0:T(8,128)S(1)} all-gather(f32[64,128]{1,0:T(8,128)S(1)} %convolution_subtract_fusion.1), channel_id=1, replica_groups=mesh['sub'=16,'row'=4,'col'=8] {'col'}, dimensions={0}, use_global_device_ids=true | all-gather | bytes 294912 | tf_op jit(solution)/shard_map/all_gather | solution.py:100
  503.8 1.3 convolution_select_fusion
  505.9 1.0 fusion.2
  (50 shorter events, 4.2 us)
Async XLA Ops:
  7.2 46.8 %all-gather.3.cloned.1.call-start = ((), (), s32[]{:S(2)}) async-start(), calls=%async_computation.2 | async-start | bytes 2621440 | tf_op jit(solution)/shard_map/all_gather | solution.py:50
  9.8 47.0 %copy-start.2 = (f32[256,512]{1,0:T(8,128)S(1)}, f32[256,512]{1,0:T(8,128)}, u32[]{:S(2)}) copy-start(f32[256,512]{1,0:T(8,128)} %bitcast_select_fusion) | copy-start | bytes 1572868
  9.8 111.4 %reduce-scatter.3.cloned.1.call-start = ((), (), s32[]{:S(2)}) async-start(), calls=%async_computation.3 | async-start | bytes 1114112 | tf_op jit(solution)/shard_map/reduce_scatter | solution.py:61
  56.8 3.8 copy-start.5
  56.8 3.8 copy-start.7
  57.8 64.3 %copy-start.6 = (s32[256]{0:T(256)S(1)}, s32[256]{0:T(256)}, u32[]{:S(2)}) copy-start(s32[256]{0:T(256)} %param.14) | copy-start | bytes 3076
  57.9 119.8 %copy-start = (f32[2,512,512]{2,1,0:T(8,128)S(1)}, f32[2,512,512]{2,1,0:T(8,128)}, u32[]{:S(2)}) copy-start(f32[2,512,512]{2,1,0:T(8,128)} %param.15) | copy-start | bytes 6291460
  60.5 107.8 %reduce-scatter.5.cloned.1.call-start = ((), (), s32[]{:S(2)}) async-start(), calls=%async_computation.5 | async-start | bytes 147456 | tf_op jit(solution)/shard_map/reduce_scatter | solution.py:90
  123.1 181.8 %all-reduce.4.cloned.1.call-start = ((), (), s32[]{:S(2)}) async-start(), calls=%async_computation.6 | async-start | bytes 131072 | tf_op jit(solution)/shard_map/psum | solution.py:11
  168.4 136.6 %copy-start.3 = (f32[32,128]{1,0:T(8,128)S(1)}, f32[32,128]{1,0:T(8,128)}, u32[]{:S(2)}) copy-start(f32[32,128]{1,0:T(8,128)} %reduce-scatter.5.cloned.1.call-done) | copy-start | bytes 49156
  179.4 165.3 %all-gather.5.cloned.1.call-start = ((), (), s32[]{:S(2)}) async-start(), calls=%async_computation.4 | async-start | bytes 1310720 | tf_op jit(solution)/shard_map/all_gather | solution.py:108
  181.4 297.9 %all-reduce.6.cloned.1.call-start = ((), (), s32[]{:S(2)}) async-start(), calls=%async_computation.7 | async-start | bytes 2228224 | tf_op jit(solution)/shard_map/psum | solution.py:11
  316.0 29.8 %copy-start.1 = (f32[128,512]{1,0:T(8,128)S(1)}, f32[128,512]{1,0:T(8,128)}, u32[]{:S(2)}) copy-start(f32[128,512]{1,0:T(8,128)} %convolution_select_fusion.1) | copy-start | bytes 786436
  479.3 26.6 %copy-start.4 = (f32[32,512]{1,0:T(8,128)S(1)}, f32[32,512]{1,0:T(8,128)}, u32[]{:S(2)}) copy-start(f32[32,512]{1,0:T(8,128)} %get-tuple-element.10) | copy-start | bytes 196612
Sparse Core Ops, SparseCore 0:
  10.1 43.8 all-gather.2
  60.7 60.4 reduce-scatter.2
  124.2 44.0 reduce-scatter.4
  179.5 125.3 all-reduce.3
  307.1 37.5 all-gather.4
  347.7 131.5 all-reduce.5
where the time goes:
time: 514 us
  waiting for transfers between devices  407 us (79%)
  blocking collectives  65.8 us (13%)
  matrix products  17.6 us (3%)
  between operations  15 us (3%)
    psum x2, waiting for transfers between devices, from_root(): return lax.psum(jnp.where(mine, value, jnp.zeros_like(value)), axis)  257 us
    reduce_scatter x1, waiting for transfers between devices, on_device(): lax.psum_scatter(contribution, 'sub', scatter_dimension=1, tiled=True)  58 us
    all_gather x2, blocking collectives, on_device(): lax.all_gather(column_slabs[panel_index], 'col', axis=0, tiled=True)  46.8 us
    all_gather x1, waiting for transfers between devices, on_device(): lax.all_gather(live_factor, 'row', axis=1, tiled=True)  43.3 us
    all_gather x1, waiting for transfers between devices, on_device(): lax.all_gather(panel_now, 'row', axis=0, tiled=True)  27 us
    reduce_scatter x1, waiting for transfers between devices, on_device(): lax.psum_scatter(jnp.dot(chooser, front_cols, precision=PRECISE), 'col',...  21.6 us
    all_gather x2, blocking collectives, on_device(): gathered = lax.all_gather(right_side, 'row', axis=1, tiled=True)  19 us
    dot_general x9, matrix products, contract(): lax.dot_general(left_part, right_part, (((left_dim,), (right_dim,)), ((),...  13.9 us
  transfers between devices with their start and end apart: 6, of which 6 were waited for; matrix products, arithmetic and copies ran while one was open for 2% of the time, Pallas kernels for 0%

commit v1 on v0

--- a/solution.py
+++ b/solution.py
@@ -6,9 +6,15 @@
 PRECISE = lax.Precision.HIGHEST
 
 
+def add_all(shard, name):
+    parts = lax.all_gather(shard, name, axis=0, tiled=False)
+    result = parts.sum(axis=0)
+    return result
+
+
 def from_root(value, axis, root):
     mine = lax.axis_index(axis) == root
-    return lax.psum(jnp.where(mine, value, jnp.zeros_like(value)), axis)
+    return add_all(jnp.where(mine, value, jnp.zeros_like(value)), axis)
 
 
 def contract(left_part, right_part, left_dim, right_dim):

time: 514 us -> 580 us (1.13)
  waiting for transfers between devices: 407 us -> 475 us
  blocking collectives: 65.8 us -> 50.7 us
  other arithmetic: 4.24 us -> 16.4 us
    all_gather x0 -> x3, waiting for transfers between devices: none -> 304 us  [add_all(): parts = lax.all_gather(shard, name, axis=0, tiled=False)]
    psum x2 -> x0, waiting for transfers between devices: 257 us -> none  [from_root(): return lax.psum(jnp.where(mine, value, jnp.zeros_like(value)), axis)]
    reduce_scatter x1, waiting for transfers between devices: 21.6 us -> 45.3 us  [on_device(): lax.psum_scatter(jnp.dot(chooser, front_cols, precision=PRECISE), 'col',...]
    all_gather x2, blocking collectives: 46.8 us -> 31.7 us  [on_device(): lax.all_gather(column_slabs[panel_index], 'col', axis=0, tiled=True)]
    reduce_sum x0 -> x3, other arithmetic: none -> 10.5 us  [add_all(): result = parts.sum(axis=0)]
  transfers between devices with their start and end apart: 6 -> 7, of which waited for: 6 -> 7; matrix products, arithmetic and copies ran while one was open for 2% -> 2% of each run, Pallas kernels for 0% -> 0%
where the time goes in v1:
time: 580 us; the launch traced here: 579 us
  waiting for transfers between devices  475 us (82%)
  blocking collectives  50.7 us (9%)
  matrix products  17.4 us (3%)
  other arithmetic  16.4 us (3%)
  between operations  15 us (3%)
    all_gather x3, waiting for transfers between devices, add_all(): parts = lax.all_gather(shard, name, axis=0, tiled=False)  304 us
    reduce_scatter x1, waiting for transfers between devices, on_device(): lax.psum_scatter(contribution, 'sub', scatter_dimension=1, tiled=True)  56.8 us
    reduce_scatter x1, waiting for transfers between devices, on_device(): lax.psum_scatter(jnp.dot(chooser, front_cols, precision=PRECISE), 'col',...  45.3 us
    all_gather x1, waiting for transfers between devices, on_device(): lax.all_gather(live_factor, 'row', axis=1, tiled=True)  43.3 us
    all_gather x2, blocking collectives, on_device(): lax.all_gather(column_slabs[panel_index], 'col', axis=0, tiled=True)  31.7 us
    all_gather x1, waiting for transfers between devices, on_device(): lax.all_gather(panel_now, 'row', axis=0, tiled=True)  24.9 us
    all_gather x2, blocking collectives, on_device(): gathered = lax.all_gather(right_side, 'row', axis=1, tiled=True)  19 us
    dot_general x9, matrix products, contract(): lax.dot_general(left_part, right_part, (((left_dim,), (right_dim,)), ((),...  13.6 us
  transfers between devices with their start and end apart: 7, of which 7 were waited for; matrix products, arithmetic and copies ran while one was open for 2% of the time, Pallas kernels for 0%

profile of v1, /device:TPU:1, one launch (start us, length us, event | category | flops | bytes accessed | tf_op | source)
XLA Modules:
  0.0 579.3 jit_solution(5218810932421864921)
XLA Ops:
  7.9 1.9 bitcast_select_fusion
  10.7 43.3 %all-gather.9.cloned.1.call-done = f32[256,2048]{1,0:T(8,128)} async-done(((f32[256,512]{1,0:T(8,128)}), f32[256,2048]{1,0:T(8,128)}) %all-gather.9.cloned.1.call-update) | async-done | bytes 2097168 | tf_op jit(solution)/shard_map/all_gather | solution.py:56
  54.0 2.8 fusion.8
  57.9 2.7 fusion
  61.9 1.1 gather_fusion
  63.1 1.1 gather_fusion.1
  64.3 56.8 %reduce-scatter.3.cloned.1.call-done = f32[128,128]{1,0:T(8,128)} async-done(((f32[128,2048]{1,0:T(8,128)}), f32[128,128]{1,0:T(8,128)}) %reduce-scatter.3.cloned.1.call-update) | async-done | bytes 65552 | tf_op jit(solution)/shard_map/reduce_scatter | solution.py:67
  123.0 45.3 %reduce-scatter.5.cloned.1.call-done = f32[32,128]{1,0:T(8,128)} async-done(((f32[256,128]{1,0:T(8,128)}), f32[32,128]{1,0:T(8,128)}) %reduce-scatter.5.cloned.1.call-update) | async-done | bytes 16400 | tf_op jit(solution)/shard_map/reduce_scatter | solution.py:96
  168.3 9.2 %all_gather.42 = f32[32,512]{1,0:T(8,128)S(1)} all-gather(f32[32,128]{1,0:T(8,128)} %reduce-scatter.5.cloned.1.call-done), channel_id=1, replica_groups=mesh['sub'=16,'row'=4,'col'=8] {'row'}, dimensions={1}, use_global_device_ids=true | all-gather | bytes 81920 | tf_op jit(solution)/shard_map/all_gather | solution.py:121
  177.5 1.7 convolution_select_fusion.3
  179.2 18.1 %all_gather.37 = f32[512,128]{1,0:T(8,128)S(1)} all-gather(f32[64,128]{1,0:T(8,128)S(1)} %unstack.10), channel_id=1, replica_groups=mesh['sub'=16,'row'=4,'col'=8] {'col'}, dimensions={0}, use_global_device_ids=true | all-gather | bytes 294912 | tf_op jit(solution)/shard_map/all_gather | solution.py:106
  197.3 2.0 convolution_select_fusion.1
  200.0 43.9 %all-gather.15.cloned.1.call-done = f32[512,512]{1,0:T(8,128)} async-done(((f32[32,512]{1,0:T(8,128)}), f32[512,512]{1,0:T(8,128)}) %all-gather.15.cloned.1.call-update) | async-done | bytes 1048592 | tf_op jit(solution)/shard_map/all_gather | solution.py:10
  243.9 1.3 reduce_sum.38
  245.2 1.3 fusion.3
  246.6 9.8 %all_gather.45 = f32[32,512]{1,0:T(8,128)S(1)} all-gather(f32[32,128]{1,0:T(8,128)S(1)} %fusion.3), channel_id=1, replica_groups=mesh['sub'=16,'row'=4,'col'=8] {'row'}, dimensions={1}, use_global_device_ids=true | all-gather | bytes 81920 | tf_op jit(solution)/shard_map/all_gather | solution.py:121
  256.3 1.7 convolution_select_fusion.2
  258.3 24.9 %all-gather.11.cloned.1.call-done = f32[512,512]{1,0:T(8,128)} async-done(((f32[128,512]{1,0:T(8,128)}), f32[512,512]{1,0:T(8,128)}) %all-gather.11.cloned.1.call-update) | async-done | bytes 1048592 | tf_op jit(solution)/shard_map/all_gather | solution.py:114
  285.0 63.0 %all-gather.17.cloned.1.call-done = f32[512,512]{1,0:T(8,128)} async-done(((f32[32,512]{1,0:T(8,128)}), f32[512,512]{1,0:T(8,128)}) %all-gather.17.cloned.1.call-update) | async-done | bytes 1048592 | tf_op jit(solution)/shard_map/all_gather | solution.py:10
  348.0 1.3 reduce_sum.39
  349.3 197.4 %all-gather.13.cloned.1.call-done = f32[8192,512]{1,0:T(8,128)} async-done(((f32[512,512]{1,0:T(8,128)}), f32[8192,512]{1,0:T(8,128)}) %all-gather.13.cloned.1.call-update) | async-done | bytes 16777232 | tf_op jit(solution)/shard_map/all_gather | solution.py:10
  546.6 7.9 %reduce_sum.37 = f32[512,512]{1,0:T(8,128)S(1)} reduce(f32[16,512,512]{2,1,0:T(8,128)} %bitcast.46, f32[]{:T(128)} %constant.128.clone.1), dimensions={0}, to_apply=%region_2.4 | reduce | flops 3932160 | bytes 17825796 | tf_op jit(solution)/shard_map/reduce_sum | solution.py:11
  555.0 13.7 %all_gather.41 = f32[512,128]{1,0:T(8,128)S(1)} all-gather(f32[64,128]{1,0:T(8,128)S(1)} %convolution_subtract_fusion.1), channel_id=1, replica_groups=mesh['sub'=16,'row'=4,'col'=8] {'col'}, dimensions={0}, use_global_device_ids=true | all-gather | bytes 294912 | tf_op jit(solution)/shard_map/all_gather | solution.py:106
  568.6 2.0 convolution_select_fusion
  (60 shorter events, 10.2 us)
Async XLA Ops:
  7.2 46.8 %all-gather.9.cloned.1.call-start = ((), (), s32[]{:S(2)}) async-start(), calls=%async_computation.2 | async-start | bytes 2621440 | tf_op jit(solution)/shard_map/all_gather | solution.py:56
  9.8 47.0 %copy-start.2 = (f32[256,512]{1,0:T(8,128)S(1)}, f32[256,512]{1,0:T(8,128)}, u32[]{:S(2)}) copy-start(f32[256,512]{1,0:T(8,128)} %bitcast_select_fusion) | copy-start | bytes 1572868
  9.8 111.2 %reduce-scatter.3.cloned.1.call-start = ((), (), s32[]{:S(2)}) async-start(), calls=%async_computation.3 | async-start | bytes 1114112 | tf_op jit(solution)/shard_map/reduce_scatter | solution.py:67
  56.8 4.9 copy-start.5
  56.8 4.9 copy-start.9
  57.8 64.1 %copy-start.8 = (s32[256]{0:T(256)S(1)}, s32[256]{0:T(256)}, u32[]{:S(2)}) copy-start(s32[256]{0:T(256)} %param.14) | copy-start | bytes 3076
  57.9 119.6 %copy-start = (f32[2,512,512]{2,1,0:T(8,128)S(1)}, f32[2,512,512]{2,1,0:T(8,128)}, u32[]{:S(2)}) copy-start(f32[2,512,512]{2,1,0:T(8,128)} %param.15) | copy-start | bytes 6291460
  60.5 107.8 %reduce-scatter.5.cloned.1.call-start = ((), (), s32[]{:S(2)}) async-start(), calls=%async_computation.5 | async-start | bytes 147456 | tf_op jit(solution)/shard_map/reduce_scatter | solution.py:96
  122.9 121.0 %all-gather.15.cloned.1.call-start = ((), (), s32[]{:S(2)}) async-start(), calls=%async_computation.7 | async-start | bytes 1114112 | tf_op jit(solution)/shard_map/all_gather | solution.py:10
  177.5 67.7 %copy-start.4 = (f32[32,128]{1,0:T(8,128)S(1)}, f32[32,128]{1,0:T(8,128)}, u32[]{:S(2)}) copy-start(f32[32,128]{1,0:T(8,128)} %reduce-scatter.5.cloned.1.call-done) | copy-start | bytes 49156
  179.2 104.0 %all-gather.11.cloned.1.call-start = ((), (), s32[]{:S(2)}) async-start(), calls=%async_computation.4 | async-start | bytes 1310720 | tf_op jit(solution)/shard_map/all_gather | solution.py:114
  199.4 148.6 %all-gather.17.cloned.1.call-start = ((), (), s32[]{:S(2)}) async-start(), calls=%async_computation.8 | async-start | bytes 1114112 | tf_op jit(solution)/shard_map/all_gather | solution.py:10
  256.3 27.9 %copy-start.1 = (f32[128,512]{1,0:T(8,128)S(1)}, f32[128,512]{1,0:T(8,128)}, u32[]{:S(2)}) copy-start(f32[128,512]{1,0:T(8,128)} %convolution_select_fusion.1) | copy-start | bytes 786436
  258.0 288.6 %all-gather.13.cloned.1.call-start = ((), (), s32[]{:S(2)}) async-start(), calls=%async_computation.6 | async-start | bytes 17825792 | tf_op jit(solution)/shard_map/all_gather | solution.py:10
  554.5 16.1 %copy-start.3 = (f32[1,64,128]{1,2,0:T(8,128)S(1)}, f32[1,64,128]{1,2,0:T(8,128)}, u32[]{:S(2)}) copy-start(f32[1,64,128]{1,2,0:T(8,128)} %dynamic-slice_bitcast_fusion.1) | copy-start | bytes 98308
  555.0 16.5 %copy-start.6 = (pred[128]{0:T(512)(128)(4,1)S(1)}, pred[128]{0:T(512)(128)(4,1)}, u32[]{:S(2)}) copy-start(pred[128]{0:T(512)(128)(4,1)} %get-tuple-element.9) | copy-start | bytes 388
  555.0 16.5 %copy-start.7 = (pred[128]{0:T(512)(128)(4,1)S(1)}, pred[128]{0:T(512)(128)(4,1)}, u32[]{:S(2)}) copy-start(pred[128]{0:T(512)(128)(4,1)} %get-tuple-element.14) | copy-start | bytes 388
Sparse Core Ops, SparseCore 0:
  10.1 43.8 all-gather.8
  60.7 60.3 reduce-scatter.2
  124.0 44.2 reduce-scatter.4
  179.3 64.5 all-gather.14
  245.9 37.2 all-gather.10
  285.1 62.8 all-gather.16
  350.0 196.5 all-gather.12
